TPU v7x, 256 devices: a whole 4x4x8 slice. The times are simulated.
256 devices in a mesh: lon: 32 (over y, z), lat: 8 (over x, core).
Axes of the slice: x: 4, y: 4, z: 8, core: 2. Of those that a mesh axis runs over, the one named last changes fastest.
Arguments:
- height: float32 [1024, 512, 1024], P(None, 'lon', 'lat'), may hold values from -1 to 1
- land_sea: int32 [512, 1024], P('lon', 'lat'), may hold values 0 or 1
- patterns: bfloat16 [512, 2, 512, 1024], P(None, None, 'lon', 'lat'), may hold values from -0.01171875 to 0.01171875
Outputs:
- covariance: float32 [32, 512, 512], P('lon', 'lat')
All inputs are finite; a program needn't handle non-finite values. No bound on the sum of `land_sea` on one device may be relied on, other than what follows from the above.
Results may differ from a plain program's by a relative error of at most 0.0003.
The roundings to bfloat16 on the way count: a program that leaves them out, or rounds other values in their place, can miss the bound.
Values sent between devices are 32-bit elements; how exact they have to be, the bound alone decides.
A program may use at most 128 MiB of HBM per device.

v0:
```python
import math

import jax
import jax.numpy as jnp
from jax import lax
from jax.sharding import PartitionSpec as P

LAG_DEV = 1


GRAVITY = 9.81
ROTATION = 7.2921e-05
EARTH_RADIUS = 6371000.0
LAT_SOUTH = 20.0
LAT_SPAN = 45.0
LON_STEP = 1.0 / 12.0


def padded_2(shard, sides, width):
    for axis, dim in sides:
        devices, length = (lax.axis_size(axis), shard.shape[dim])
        up = [(i, (i + 1) % devices) for i in range(devices - 1)]
        down = [(j, i) for i, j in up]
        last = lax.slice_in_dim(shard, length - width, length, axis=dim)
        initial = lax.slice_in_dim(shard, 0, width, axis=dim)
        before = lax.ppermute(last, axis, up)
        after = lax.ppermute(initial, axis, down)
        shard = jnp.concatenate([before, shard, after], axis=dim)
    return shard


def stencil_coefs(rows_index, total_rows):
    degrees = LAT_SOUTH + LAT_SPAN * (rows_index.astype(jnp.float32) + 0.5) / total_rows
    radians = degrees * (math.pi / 180.0)
    coriolis = 2.0 * ROTATION * jnp.sin(radians)
    north_step = EARTH_RADIUS * (LAT_SPAN / total_rows) * (math.pi / 180.0)
    east_step = EARTH_RADIUS * jnp.cos(radians) * (LON_STEP * math.pi / 180.0)
    return (-GRAVITY / (coriolis * 2.0 * north_step), GRAVITY / (coriolis * 2.0 * east_step))


def velocities(padded, coef_east, coef_north, ocean):
    lat_diff = padded[:, 1:-1, 2:] - padded[:, 1:-1, :-2]
    lon_diff = padded[:, 2:, 1:-1] - padded[:, :-2, 1:-1]
    return (coef_east * lat_diff * ocean, coef_north * lon_diff * ocean)


def on_device(height, land_sea, patterns):
    days, lon_cells, lat_cells = height.shape
    lat_devices = lax.axis_size("lat")
    lon_devices = lax.axis_size("lon")
    total_rows = lat_cells * lat_devices
    lat_place = lax.axis_index("lat")
    lon_place = lax.axis_index("lon")
    rows_index = lat_place * lat_cells + jnp.arange(lat_cells, dtype=jnp.int32)
    coef_east, coef_north = stencil_coefs(rows_index, total_rows)
    ocean = land_sea.astype(jnp.float32)
    padded = padded_2(height, (("lon", 1), ("lat", 2)), 1)
    east_vel, north_vel = velocities(padded, coef_east, coef_north, ocean)
    local_energy = jnp.sum(east_vel * east_vel + north_vel * north_vel)
    stacked = (
        jnp.stack([east_vel, north_vel], axis=1)
        .astype(jnp.bfloat16)
        .reshape(days, 2 * lon_cells * lat_cells)
    )
    mode_count = patterns.shape[0]
    owned = mode_count // lat_devices
    flat_patterns = patterns.reshape(mode_count, 2 * lon_cells * lat_cells)
    energy = lax.psum(local_energy, ("lon", "lat"))
    totals = lax.psum(
        lax.dot_general(
            flat_patterns, stacked, (((1,), (1,)), ((), ())), preferred_element_type=jnp.float32
        ),
        ("lon", "lat"),
    )
    cell_total = 2.0 * days * lon_cells * lon_devices * total_rows
    centered = totals - jnp.mean(totals, axis=1, keepdims=True)
    normed = centered / jnp.sqrt(energy / cell_total + 1e-06)
    my_rows = lax.dynamic_slice_in_dim(normed, lat_place * owned, owned, 0)
    padded_rows = jnp.concatenate([my_rows, jnp.zeros_like(my_rows)], axis=1)
    lag = lon_place * LAG_DEV + 0
    shifted = lax.dynamic_slice_in_dim(padded_rows, lag, days, 1)
    product = lax.dot_general(
        shifted,
        normed,
        (((1,), (1,)), ((), ())),
        precision=lax.Precision.HIGHEST,
        preferred_element_type=jnp.float32,
    )
    results = [product / (days - lag).astype(jnp.float32)]
    return jnp.stack(results, axis=0)


def solution(mesh):
    placed = (P(None, "lon", "lat"), P("lon", "lat"), P(None, None, "lon", "lat"))
    return jax.shard_map(
        on_device, mesh=mesh, in_specs=placed, out_specs=P("lon", "lat", None), check_vma=False
    )
```

profile of v0, /device:TPU:1, one launch (start us, length us, event | category | flops | bytes accessed | tf_op | source)
XLA Modules:
  0.0 380.6 jit_solution(7635947852473987990)
XLA Ops:
  6.5 0.0 copy-start.2
  6.5 0.0 all-reduce.3.cloned.1.call-start
  6.5 6.1 %copy.10 = f32[1024,16,128]{2,0,1:T(8,128)S(1)} copy(f32[1024,16,128]{2,1,0:T(8,128)} %param.3) | data formatting | bytes 16777216 | tf_op args[0]
  12.6 0.0 copy-start.1
  12.6 3.3 copy-done.1
  15.9 0.1 fusion.23
  16.0 4.4 %collective-permute-start = (f32[1024,1,128]{2,0,1:T(8,128)S(1)}, f32[1024,1,128]{2,0,1:T(8,128)S(1)}, u32[]{:S(2)}, u32[]{:S(2)}) collective-permute-start(f32[1024,1,128]{2,0,1:T(8,128)S(1)} %get-tuple-element.11), channel_id=1, source_target_pairs={{0,8},{8,16},{16,24},{24,32},{32,40},{40,48},{48,56},{56,64},{64,7... | collective-permute-start | bytes 1572872 | tf_op jit(solution)/shard_map/ppermute | solution.py:26
  20.4 1.3 collective-permute-start.1
  21.7 0.0 copy-done.2
  21.7 9.2 %collective-permute-done = f32[1024,1,128]{2,0,1:T(8,128)S(1)} collective-permute-done((f32[1024,1,128]{2,0,1:T(8,128)S(1)}, f32[1024,1,128]{2,0,1:T(8,128)S(1)}, u32[]{:S(2)}, u32[]{:S(2)}) %collective-permute-start) | collective-permute-done | bytes 524320 | tf_op jit(solution)/shard_map/ppermute | solution.py:26
  31.0 5.8 %constant_dynamic-update-slice_fusion.1 = f32[1024,18,128]{2,0,1:T(8,128)S(1)} fusion(f32[1024,18,128]{2,0,1:T(8,128)S(1)} %constant_dynamic-update-slice_fusion.2, f32[1024,16,128]{2,1,0:T(8,128)} %param.3), kind=kLoop, calls=%fused_computation.24 | loop fusion | bytes 16777216
  36.8 0.0 collective-permute-done.1
  36.9 0.0 copy-start
  36.9 8.4 %fusion.22 = (f32[1024,18,1]{2,0,1:T(8,128)}, f32[1024,18,1]{2,0,1:T(8,128)}) fusion(f32[1024,18,128]{2,0,1:T(8,128)S(1)} %constant_dynamic-update-slice_fusion), kind=kLoop, calls=%fused_computation.35 | loop fusion | bytes 294912 | tf_op jit(solution)/shard_map/slice | solution.py:25
  45.3 0.9 copy-done
  46.1 5.6 %copy.13 = f32[1024,18,1]{0,2,1:T(1,128)S(1)} copy(f32[1024,18,1]{2,0,1:T(8,128)} %get-tuple-element.8) | data formatting | bytes 147456 | tf_op jit(solution)/shard_map/slice | solution.py:25
  51.7 3.4 collective-permute-start.2
  55.2 5.6 %copy.15 = f32[1024,18,1]{0,2,1:T(1,128)S(1)} copy(f32[1024,18,1]{2,0,1:T(8,128)} %get-tuple-element.9) | data formatting | bytes 147456 | tf_op jit(solution)/shard_map/slice | solution.py:24
  60.8 3.2 collective-permute-start.3
  64.0 0.1 multiply_divide_fusion
  64.1 0.0 collective-permute-done.2
  64.1 5.1 %copy.14 = f32[1024,18,1]{2,0,1:T(8,128)} copy(f32[1024,18,1]{0,2,1:T(1,128)S(1)} %collective-permute-done.2) | data formatting | bytes 147456 | tf_op jit(solution)/shard_map/ppermute | solution.py:27
  69.2 0.0 collective-permute-done.3
  69.2 5.2 %copy.16 = f32[1024,18,1]{2,0,1:T(8,128)} copy(f32[1024,18,1]{0,2,1:T(1,128)S(1)} %collective-permute-done.3) | data formatting | bytes 147456 | tf_op jit(solution)/shard_map/ppermute | solution.py:26
  74.3 18.3 %add_reduce_fusion = (f32[]{:T(128)}, bf16[1024,16,128]{2,0,1:T(8,128)(2,1)S(1)}, bf16[1024,1,16,128]{3,0,2,1:T(8,128)(2,1)S(1)}) fusion(f32[16,128]{1,0:T(8,128)S(1)} %convert_element_type.18, f32[1024,16,128]{2,0,1:T(8,128)} %copy-done.1, f32[1024,1,128]{2,0,1:T(8,128)S(1)} %collective-permute-done, f32[1024,1,128]{2,0,1:T(8,128)S(1)} %collective-permute-done.1, ...), kind=kLoop, calls=%fused_computation.14 | loop fusion | flops 33554432 | bytes 27419652 | tf_op jit(solution)/shard_map/reduce_sum | solution.py:59
  92.6 8.1 %fusion.11 = f32[512,1024]{0,1:T(8,128)} fusion(bf16[512,2,16,128]{3,2,1,0:T(8,128)(2,1)} %param.5, bf16[1024,1,16,128]{3,0,2,1:T(8,128)(2,1)S(1)} %get-tuple-element.7, bf16[1024,1,16,128]{3,0,2,1:T(8,128)(2,1)S(1)} %bitcast.14), kind=kOutput, calls=%fused_computation.19 | convolution fusion | flops 4299161600 | bytes 14680064 | tf_op jit(solution)/shard_map/dot_general | solution.py:70
  100.7 0.0 all-reduce.3.cloned.1.call-update
  100.8 80.2 %psum.15 = f32[]{:T(128)} all-reduce(f32[]{:T(128)} %get-tuple-element.5), channel_id=1, replica_groups=mesh['lon'=32,'lat'=8] {'lon','lat'}, use_global_device_ids=true, to_apply=%region_3.0 | all-reduce | flops 1 | bytes 8 | tf_op jit(solution)/shard_map/psum | solution.py:68
  181.6 186.2 %all-reduce.3.cloned.1.call-done = f32[512,1024]{0,1:T(8,128)} async-done(((f32[512,1024]{0,1:T(8,128)}), f32[512,1024]{0,1:T(8,128)}) %all-reduce.3.cloned.1.call-update) | async-done | bytes 2097168 | tf_op jit(solution)/shard_map/psum | solution.py:69
  367.8 1.8 reduce_sum.18
  369.6 1.9 subtract_divide_fusion
  371.5 0.2 constant_dynamic-slice_fusion
  371.7 2.0 fusion.16
  (4 shorter events, 0.1 us)
Async XLA Ops:
  6.5 15.2 %copy-start.2 = (s32[16,128]{1,0:T(8,128)S(1)}, s32[16,128]{1,0:T(8,128)}, u32[]{:S(2)}) copy-start(s32[16,128]{1,0:T(8,128)} %param.4) | copy-start | bytes 24580
  6.5 361.3 %all-reduce.3.cloned.1.call-start = ((), (), s32[]{:S(2)}) async-start(), calls=%async_computation | async-start | bytes 4194304 | tf_op jit(solution)/shard_map/psum | solution.py:69
  12.6 3.3 copy-start.1
  16.0 15.0 %collective-permute-start = (f32[1024,1,128]{2,0,1:T(8,128)S(1)}, f32[1024,1,128]{2,0,1:T(8,128)S(1)}, u32[]{:S(2)}, u32[]{:S(2)}) collective-permute-start(f32[1024,1,128]{2,0,1:T(8,128)S(1)} %get-tuple-element.11), channel_id=1, source_target_pairs={{0,8},{8,16},{16,24},{24,32},{32,40},{40,48},{48,56},{56,64},{64,7... | collective-permute-start | bytes 1572872 | tf_op jit(solution)/shard_map/ppermute | solution.py:26
  20.4 16.4 %collective-permute-start.1 = (f32[1024,1,128]{2,0,1:T(8,128)S(1)}, f32[1024,1,128]{2,0,1:T(8,128)S(1)}, u32[]{:S(2)}, u32[]{:S(2)}) collective-permute-start(f32[1024,1,128]{2,0,1:T(8,128)S(1)} %get-tuple-element.10), channel_id=1, source_target_pairs={{8,0},{16,8},{24,16},{32,24},{40,32},{48,40},{56,48},{64,56},{72,6... | collective-permute-start | bytes 1572872 | tf_op jit(solution)/shard_map/ppermute | solution.py:27
  36.9 9.3 %copy-start = (f32[1024,18,128]{2,0,1:T(8,128)}, f32[1024,18,128]{2,0,1:T(8,128)S(1)}, u32[]{:S(2)}) copy-start(f32[1024,18,128]{2,0,1:T(8,128)S(1)} %constant_dynamic-update-slice_fusion) | copy-start | bytes 28311556
  51.7 12.3 %collective-permute-start.2 = (f32[1024,18,1]{0,2,1:T(1,128)S(1)}, f32[1024,18,1]{0,2,1:T(1,128)S(1)}, u32[]{:S(2)}, u32[]{:S(2)}) collective-permute-start(f32[1024,18,1]{0,2,1:T(1,128)S(1)} %copy.13), channel_id=1, source_target_pairs={{1,0},{2,1},{3,2},{4,3},{5,4},{6,5},{7,6},{9,8},{10,9},{11,10},{12... | collective-permute-start | bytes 221192 | tf_op jit(solution)/shard_map/ppermute | solution.py:27
  60.8 8.4 %collective-permute-start.3 = (f32[1024,18,1]{0,2,1:T(1,128)S(1)}, f32[1024,18,1]{0,2,1:T(1,128)S(1)}, u32[]{:S(2)}, u32[]{:S(2)}) collective-permute-start(f32[1024,18,1]{0,2,1:T(1,128)S(1)} %copy.15), channel_id=1, source_target_pairs={{0,1},{1,2},{2,3},{3,4},{4,5},{5,6},{6,7},{8,9},{9,10},{10,11},{11... | collective-permute-start | bytes 221192 | tf_op jit(solution)/shard_map/ppermute | solution.py:26
Sparse Core Ops, SparseCore 0:
  100.9 266.8 all-reduce.2
where the time goes:
time: 382 us; the launch traced here: 381 us
  waiting for transfers between devices  195 us (51%)
  blocking collectives  80.2 us (21%)
  local copies, waits for them, and re-layouts  46.3 us (12%)
  other arithmetic  22 us (6%)
  between operations  14.2 us (4%)
  starting transfers between devices  12.3 us (3%)
  matrix products  10.1 us (3%)
    psum x1, waiting for transfers between devices, on_device(): lax.psum(lax.dot_general(flat_patterns, stacked, (((1,), (1,)), ((), ()))...  186 us
    psum x1, blocking collectives, on_device(): energy = lax.psum(local_energy, ('lon', 'lat'))  80.2 us
    reduce_sum x1, other arithmetic, on_device(): local_energy = jnp.sum(east_vel * east_vel + north_vel * north_vel)  18.3 us
    unnamed x9, local copies, waits for them, and re-layouts  16.1 us
    slice x3, local copies, waits for them, and re-layouts, padded_2(): initial = lax.slice_in_dim(shard, 0, width, axis=dim)  14.1 us
    ppermute x2, waiting for transfers between devices, padded_2(): before = lax.ppermute(last, axis, up)  9.23 us
    dot_general x1, matrix products, on_device(): lax.dot_general(flat_patterns, stacked, (((1,), (1,)), ((), ())), preferr...  8.1 us
  transfers between devices with their start and end apart: 5, of which 2 were waited for; matrix products, arithmetic and copies ran while one was open for 4% of the time, Pallas kernels for 0%

commit v1 on v0

--- a/solution.py
+++ b/solution.py
@@ -1,9 +1,193 @@
 import math
+
+from jax.sharding import PartitionSpec as P
 
 import jax
 import jax.numpy as jnp
 from jax import lax
-from jax.sharding import PartitionSpec as P
+from jax.experimental import pallas as pl
+from jax.experimental.pallas import tpu as pltpu
+
+MESH = pl.DeviceIdType.MESH
+
+
+def allreduce_kernel(tot, en, out, eout, rc, acc, r2, acc2, r3, acc3, r4, er, ea,
+                     s_core, v_core, s_mid, v_mid, s_z, v_z, s_e, v_e):
+    lon = lax.axis_index("lon")
+    lat = lax.axis_index("lat")
+    y, z = lon // 8, lon % 8
+    x, c = lat // 2, lat % 2
+    partner = (lon, x * 2 + (1 - c))
+
+    def at_x(d):
+        return (lon, ((x + d) % 4) * 2 + c)
+
+    def at_y(d):
+        return (((y + d) % 4) * 8 + z, lat)
+
+    def at_z(d):
+        return (y * 8 + (z + d) % 8, lat)
+
+    pending = []
+
+    def send(src, dst, ssem, rsem, dev):
+        copy = pltpu.make_async_remote_copy(
+            src_ref=src, dst_ref=dst, send_sem=ssem, recv_sem=rsem,
+            device_id=dev, device_id_type=MESH)
+        copy.start()
+        pending.append(copy)
+        return copy
+
+    barrier = pltpu.get_barrier_semaphore()
+    peers = [partner] + [at_x(d) for d in (1, 2, 3)] + [at_y(d) for d in (1, 2, 3)]
+    peers += [at_z(d) for d in range(1, 8)]
+    for dev in peers:
+        pl.semaphore_signal(barrier, inc=1, device_id=dev, device_id_type=MESH)
+    pl.semaphore_wait(barrier, len(peers))
+
+    first = (x, y)
+    second = (y, x)
+    at_first = (at_x, at_y)
+    at_second = (at_y, at_x)
+    order = (2, 1, 3, 0)
+
+    def rows_of(core, q):
+        return pl.ds(pl.multiple_of(core * 256 + q * 64, 64), 64)
+
+    lanes = (pl.ds(0, 512), pl.ds(512, 512))
+
+    e0 = send(en, er.at[0], s_e.at[0], v_e.at[0], partner)
+    core = {}
+    for d in order:
+        for h in (0, 1):
+            q = (first[h] + d) % 4
+            core[h, d] = send(tot.at[rows_of(1 - c, q), lanes[h]], rc.at[h, d],
+                              s_core.at[h * 4 + d], v_core.at[h * 4 + d], partner)
+    mid = {}
+    for d in order:
+        for h in (0, 1):
+            q = (first[h] + d) % 4
+            core[h, d].wait_recv()
+            acc[h, d] = tot[rows_of(c, q), lanes[h]] + rc[h, d]
+            if d:
+                mid[h, d] = send(acc.at[h, d], r2.at[h, d - 1], s_mid.at[h * 3 + d - 1],
+                                 v_mid.at[h * 3 + d - 1], at_first[h](d))
+    e0.wait_recv()
+    ea[0] = en[...] + er[0]
+    ex = [send(ea.at[0], er.at[d], s_e.at[d], v_e.at[d], at_x(d)) for d in (1, 2, 3)]
+    mid2 = {}
+    for h in (0, 1):
+        for d in (1, 3, 2):
+            mid[h, d].wait_recv()
+        acc2[h] = (acc[h, 0] + r2[h, 0]) + (r2[h, 1] + r2[h, 2])
+        for d in (2, 1, 3):
+            q = (second[h] + d) % 4
+            mid2[h, d] = send(acc2.at[h, pl.ds(pl.multiple_of(q * 16, 16), 16)], r3.at[h, d - 1],
+                              s_mid.at[6 + h * 3 + d - 1], v_mid.at[6 + h * 3 + d - 1],
+                              at_second[h](d))
+    for copy in ex:
+        copy.wait_recv()
+    ea[1] = (ea[0] + er[1]) + (er[2] + er[3])
+    ey = [send(ea.at[1], er.at[3 + d], s_e.at[3 + d], v_e.at[3 + d], at_y(d)) for d in (1, 2, 3)]
+    zorder = (4, 3, 5, 2, 6, 1, 7)
+    zc = {}
+
+    def zblock(zq):
+        return pl.ds(pl.multiple_of((zq // 4) * 8, 8), 8), zq % 4
+
+    for h in (0, 1):
+        for d in (1, 3, 2):
+            mid2[h, d].wait_recv()
+        acc3[h] = (acc2[h, pl.ds(pl.multiple_of(second[h] * 16, 16), 16)] + r3[h, 0]) + (
+            r3[h, 1] + r3[h, 2])
+        for d in zorder:
+            r, l = zblock((z + d) % 8)
+            zc[h, d] = send(acc3.at[h, r, pl.ds(pl.multiple_of(l * 128, 128), 128)],
+                            r4.at[h, d - 1], s_z.at[h * 7 + d - 1], v_z.at[h * 7 + d - 1], at_z(d))
+    for copy in ey:
+        copy.wait_recv()
+    ea[2] = (ea[1] + er[4]) + (er[5] + er[6])
+    ez = [send(ea.at[2], er.at[6 + d], s_e.at[6 + d], v_e.at[6 + d], at_z(d)) for d in range(1, 8)]
+
+    base = [pl.multiple_of(c * 256 + first[h] * 64 + second[h] * 16, 16) for h in (0, 1)]
+    gz = {}
+    for h in (0, 1):
+        for d in (1, 7, 2, 6, 3, 5, 4):
+            zc[h, d].wait_recv()
+        r, l = zblock(z)
+        mine = acc3[h, r, pl.ds(pl.multiple_of(l * 128, 128), 128)]
+        mine = ((mine + r4[h, 0]) + (r4[h, 1] + r4[h, 2])) + (
+            (r4[h, 3] + r4[h, 4]) + (r4[h, 5] + r4[h, 6]))
+        place = (pl.ds(pl.multiple_of(base[h] + (z // 4) * 8, 8), 8),
+                 pl.ds(pl.multiple_of(h * 512 + l * 128, 128), 128))
+        out[place] = mine
+        for d in zorder:
+            gz[h, d] = send(out.at[place], out.at[place], s_z.at[14 + h * 7 + d - 1],
+                            v_z.at[14 + h * 7 + d - 1], at_z(d))
+    for copy in ez:
+        copy.wait_recv()
+    total = ea[2]
+    for d in range(1, 8):
+        total = total + er[6 + d]
+    eout[...] = total
+
+    g2 = {}
+    for h in (0, 1):
+        for d in (1, 7, 2, 6, 3, 5, 4):
+            gz[h, d].wait_recv()
+        region = out.at[pl.ds(base[h], 16), lanes[h]]
+        for d in (2, 1, 3):
+            g2[h, d] = send(region, region, s_mid.at[12 + h * 3 + d - 1],
+                            v_mid.at[12 + h * 3 + d - 1], at_second[h](d))
+    g1 = {}
+    gc = {}
+    for h in (0, 1):
+        for d in (1, 3, 2):
+            g2[h, d].wait_recv()
+        region = out.at[rows_of(c, first[h]), lanes[h]]
+        for d in (2, 1, 3):
+            g1[h, d] = send(region, region, s_mid.at[18 + h * 3 + d - 1],
+                            v_mid.at[18 + h * 3 + d - 1], at_first[h](d))
+        gc[h, 0] = send(region, region, s_core.at[8 + h * 4], v_core.at[8 + h * 4], partner)
+    for d in (1, 3, 2):
+        for h in (0, 1):
+            g1[h, d].wait_recv()
+            region = out.at[rows_of(c, (first[h] + 4 - d) % 4), lanes[h]]
+            gc[h, d] = send(region, region, s_core.at[8 + h * 4 + d], v_core.at[8 + h * 4 + d],
+                            partner)
+    for d in (0, 1, 3, 2):
+        for h in (0, 1):
+            gc[h, d].wait_recv()
+    for copy in pending:
+        copy.wait_send()
+
+
+def allreduce(tot, en, collective_id=0):
+    f32 = jnp.float32
+    vm = pl.BlockSpec(memory_space=pltpu.VMEM)
+    return pl.pallas_call(
+        allreduce_kernel,
+        out_shape=[jax.ShapeDtypeStruct((512, 1024), f32), jax.ShapeDtypeStruct((8, 128), f32)],
+        in_specs=[vm, vm],
+        out_specs=[vm, vm],
+        scratch_shapes=[
+            pltpu.VMEM((2, 4, 64, 512), f32),
+            pltpu.VMEM((2, 4, 64, 512), f32),
+            pltpu.VMEM((2, 3, 64, 512), f32),
+            pltpu.VMEM((2, 64, 512), f32),
+            pltpu.VMEM((2, 3, 16, 512), f32),
+            pltpu.VMEM((2, 16, 512), f32),
+            pltpu.VMEM((2, 7, 8, 128), f32),
+            pltpu.VMEM((14, 8, 128), f32),
+            pltpu.VMEM((3, 8, 128), f32),
+            pltpu.SemaphoreType.DMA((16,)), pltpu.SemaphoreType.DMA((16,)),
+            pltpu.SemaphoreType.DMA((24,)), pltpu.SemaphoreType.DMA((24,)),
+            pltpu.SemaphoreType.DMA((28,)), pltpu.SemaphoreType.DMA((28,)),
+            pltpu.SemaphoreType.DMA((14,)), pltpu.SemaphoreType.DMA((14,)),
+        ],
+        compiler_params=pltpu.CompilerParams(collective_id=collective_id, has_side_effects=True),
+    )(tot, en)
+
 
 LAG_DEV = 1
 
@@ -65,13 +249,11 @@
     mode_count = patterns.shape[0]
     owned = mode_count // lat_devices
     flat_patterns = patterns.reshape(mode_count, 2 * lon_cells * lat_cells)
-    energy = lax.psum(local_energy, ("lon", "lat"))
-    totals = lax.psum(
-        lax.dot_general(
-            flat_patterns, stacked, (((1,), (1,)), ((), ())), preferred_element_type=jnp.float32
-        ),
-        ("lon", "lat"),
-    )
+    part = lax.dot_general(
+        flat_patterns, stacked, (((1,), (1,)), ((), ())), preferred_element_type=jnp.float32
+    )
+    totals, energies = allreduce(part, jnp.full((8, 128), local_energy * (1.0 / 1024.0)))
+    energy = jnp.sum(energies)
     cell_total = 2.0 * days * lon_cells * lon_devices * total_rows
     centered = totals - jnp.mean(totals, axis=1, keepdims=True)
     normed = centered / jnp.sqrt(energy / cell_total + 1e-06)

time: 382 us -> 161 us (0.42)
  waiting for transfers between devices: 195 us -> 9.23 us
  blocking collectives: 80.2 us -> 0 us
  Pallas kernels: 0 us -> 50.3 us
  between operations: 14.2 us -> 1.49 us
  other arithmetic: 22 us -> 26.8 us
    psum x1 -> x0, waiting for transfers between devices: 186 us -> none  [on_device(): lax.psum(lax.dot_general(flat_patterns, stacked, (((1,), (1,)), ((), ()))...]
    psum x1 -> x0, blocking collectives: 80.2 us -> none  [on_device(): energy = lax.psum(local_energy, ('lon', 'lat'))]
    pallas_call x0 -> x1, Pallas kernels: none -> 50.3 us  [allreduce(): pl.pallas_call(allreduce_kernel, out_shape=[jax.ShapeDtypeStruct((512, 10...]
  transfers between devices with their start and end apart: 5 -> 4, of which waited for: 2 -> 1; matrix products, arithmetic and copies ran while one was open for 4% -> 10% of each run, Pallas kernels for 0% -> 0%
where the time goes in v1:
time: 161 us; the launch traced here: 160 us
  Pallas kernels  50.3 us (31%)
  local copies, waits for them, and re-layouts  46.6 us (29%)
  other arithmetic  26.8 us (17%)
  matrix products  13.4 us (8%)
  starting transfers between devices  12.3 us (8%)
  waiting for transfers between devices  9.23 us (6%)
    pallas_call x1, Pallas kernels, allreduce(): pl.pallas_call(allreduce_kernel, out_shape=[jax.ShapeDtypeStruct((512, 10...  50.3 us
    reduce_sum x1, other arithmetic, on_device(): local_energy = jnp.sum(east_vel * east_vel + north_vel * north_vel)  21.8 us
    unnamed x9, local copies, waits for them, and re-layouts  16.1 us
    slice x3, local copies, waits for them, and re-layouts, padded_2(): initial = lax.slice_in_dim(shard, 0, width, axis=dim)  14.1 us
    dot_general x1, matrix products, on_device(): lax.dot_general(flat_patterns, stacked, (((1,), (1,)), ((), ())), preferr...  10.6 us
    ppermute x2, waiting for transfers between devices, padded_2(): before = lax.ppermute(last, axis, up)  9.22 us
    ppermute x2, starting transfers between devices, padded_2(): before = lax.ppermute(last, axis, up)  7.59 us
    slice x1, local copies, waits for them, and re-layouts, padded_2(): last = lax.slice_in_dim(shard, length - width, length, axis=dim)  5.62 us
  transfers between devices with their start and end apart: 4, of which 1 were waited for; matrix products, arithmetic and copies ran while one was open for 10% of the time, Pallas kernels for 0%

profile of v1, /device:TPU:1, one launch (start us, length us, event | category | flops | bytes accessed | tf_op | source)
XLA Modules:
  0.0 160.2 jit_solution(3683163807503451549)
XLA Ops:
  0.0 0.0 copy-start.2
  0.0 6.1 %copy.11 = f32[1024,16,128]{2,0,1:T(8,128)S(1)} copy(f32[1024,16,128]{2,1,0:T(8,128)} %param.3) | data formatting | bytes 16777216 | tf_op args[0]
  6.1 0.0 copy-start.1
  6.1 3.3 %copy-done.1 = f32[1024,16,128]{2,0,1:T(8,128)} copy-done((f32[1024,16,128]{2,0,1:T(8,128)}, f32[1024,16,128]{2,0,1:T(8,128)S(1)}, u32[]{:S(2)}) %copy-start.1) | copy-done | bytes 8388632
  9.4 0.1 fusion.23
  9.5 4.4 %collective-permute-start = (f32[1024,1,128]{2,0,1:T(8,128)S(1)}, f32[1024,1,128]{2,0,1:T(8,128)S(1)}, u32[]{:S(2)}, u32[]{:S(2)}) collective-permute-start(f32[1024,1,128]{2,0,1:T(8,128)S(1)} %get-tuple-element.15), channel_id=1, source_target_pairs={{0,8},{8,16},{16,24},{24,32},{32,40},{40,48},{48,56},{56,64},{64,7... | collective-permute-start | bytes 1572872 | tf_op jit(solution)/shard_map/ppermute | solution.py:210
  13.9 1.3 collective-permute-start.1
  15.2 0.0 copy-done.2
  15.2 9.2 %collective-permute-done = f32[1024,1,128]{2,0,1:T(8,128)S(1)} collective-permute-done((f32[1024,1,128]{2,0,1:T(8,128)S(1)}, f32[1024,1,128]{2,0,1:T(8,128)S(1)}, u32[]{:S(2)}, u32[]{:S(2)}) %collective-permute-start) | collective-permute-done | bytes 524320 | tf_op jit(solution)/shard_map/ppermute | solution.py:210
  24.5 5.8 %constant_dynamic-update-slice_fusion.1 = f32[1024,18,128]{2,0,1:T(8,128)S(1)} fusion(f32[1024,18,128]{2,0,1:T(8,128)S(1)} %constant_dynamic-update-slice_fusion.2, f32[1024,16,128]{2,1,0:T(8,128)} %param.3), kind=kLoop, calls=%fused_computation.24 | loop fusion | bytes 16777216
  30.3 0.0 collective-permute-done.1
  30.3 0.0 copy-start
  30.3 8.4 %fusion.22 = (f32[1024,18,1]{2,0,1:T(8,128)}, f32[1024,18,1]{2,0,1:T(8,128)}) fusion(f32[1024,18,128]{2,0,1:T(8,128)S(1)} %constant_dynamic-update-slice_fusion), kind=kLoop, calls=%fused_computation.35 | loop fusion | bytes 294912 | tf_op jit(solution)/shard_map/slice | solution.py:209
  38.7 0.9 copy-done
  39.6 5.6 %copy.14 = f32[1024,18,1]{0,2,1:T(1,128)S(1)} copy(f32[1024,18,1]{2,0,1:T(8,128)} %get-tuple-element.12) | data formatting | bytes 147456 | tf_op jit(solution)/shard_map/slice | solution.py:209
  45.2 3.4 %collective-permute-start.2 = (f32[1024,18,1]{0,2,1:T(1,128)S(1)}, f32[1024,18,1]{0,2,1:T(1,128)S(1)}, u32[]{:S(2)}, u32[]{:S(2)}) collective-permute-start(f32[1024,18,1]{0,2,1:T(1,128)S(1)} %copy.14), channel_id=1, source_target_pairs={{1,0},{2,1},{3,2},{4,3},{5,4},{6,5},{7,6},{9,8},{10,9},{11,10},{12... | collective-permute-start | bytes 221192 | tf_op jit(solution)/shard_map/ppermute | solution.py:211
  48.6 5.6 %copy.16 = f32[1024,18,1]{0,2,1:T(1,128)S(1)} copy(f32[1024,18,1]{2,0,1:T(8,128)} %get-tuple-element.13) | data formatting | bytes 147456 | tf_op jit(solution)/shard_map/slice | solution.py:208
  54.3 3.2 %collective-permute-start.3 = (f32[1024,18,1]{0,2,1:T(1,128)S(1)}, f32[1024,18,1]{0,2,1:T(1,128)S(1)}, u32[]{:S(2)}, u32[]{:S(2)}) collective-permute-start(f32[1024,18,1]{0,2,1:T(1,128)S(1)} %copy.16), channel_id=1, source_target_pairs={{0,1},{1,2},{2,3},{3,4},{4,5},{5,6},{6,7},{8,9},{9,10},{10,11},{11... | collective-permute-start | bytes 221192 | tf_op jit(solution)/shard_map/ppermute | solution.py:210
  57.5 0.1 multiply_divide_fusion
  57.5 0.0 collective-permute-done.2
  57.5 5.1 %copy.15 = f32[1024,18,1]{2,0,1:T(8,128)} copy(f32[1024,18,1]{0,2,1:T(1,128)S(1)} %collective-permute-done.2) | data formatting | bytes 147456 | tf_op jit(solution)/shard_map/ppermute | solution.py:211
  62.6 0.0 collective-permute-done.3
  62.6 5.1 %copy.17 = f32[1024,18,1]{2,0,1:T(8,128)} copy(f32[1024,18,1]{0,2,1:T(1,128)S(1)} %collective-permute-done.3) | data formatting | bytes 147456 | tf_op jit(solution)/shard_map/ppermute | solution.py:210
  67.7 21.8 %add_reduce_fusion = (f32[]{:T(128)}, bf16[1024,16,128]{2,0,1:T(8,128)(2,1)}, bf16[1024,1,16,128]{3,0,2,1:T(8,128)(2,1)}) fusion(f32[16,128]{1,0:T(8,128)S(1)} %convert_element_type.18, f32[1024,16,128]{2,0,1:T(8,128)} %copy-done.1, f32[1024,1,128]{2,0,1:T(8,128)S(1)} %collective-permute-done, f32[1024,1,128]{2,0,1:T(8,128)S(1)} %collective-permute-done.1, ...), kind=kLoop, calls=%fused_computation.14 | loop fusion | flops 33554432 | bytes 27419652 | tf_op jit(solution)/shard_map/reduce_sum | solution.py:243
  90.2 10.6 %fusion.11.tot = f32[512,1024]{1,0:T(8,128)} fusion(bf16[512,2,16,128]{3,2,1,0:T(8,128)(2,1)} %param.5, bf16[1024,1,16,128]{3,0,2,1:T(8,128)(2,1)} %get-tuple-element.11, bf16[1024,1,16,128]{3,0,2,1:T(8,128)(2,1)} %bitcast.12), kind=kOutput, calls=%fused_computation.19 | convolution fusion | flops 4299161600 | bytes 14680064 | tf_op jit(solution)/shard_map/dot_general | solution.py:252
  100.8 0.6 broadcast_in_dim.2.en
  101.4 50.3 %shard_map.37 = (f32[512,1024]{1,0:T(8,128)}, f32[8,128]{1,0:T(8,128)}) custom-call(f32[512,1024]{1,0:T(8,128)} %fusion.11.tot, f32[8,128]{1,0:T(8,128)} %broadcast_in_dim.2.en), custom_call_target="tpu_custom_call" | custom-call | tf_op jit(solution)/shard_map/pallas_call | solution.py:168
  151.7 1.8 %reduce_sum.28 = f32[512]{0:T(512)S(1)} reduce(f32[512,1024]{1,0:T(8,128)} %get-tuple-element.7, f32[]{:T(128)} %constant.17.clone.1), dimensions={1}, to_apply=%region_1.0 | reduce | flops 523776 | bytes 2099204 | tf_op jit(solution)/shard_map/reduce_sum | solution.py:258
  153.5 1.3 reduce_sum.29
  155.5 1.8 %subtract_divide_fusion = f32[512,1024]{1,0:T(8,128)S(1)} fusion(f32[512,1024]{1,0:T(8,128)} %get-tuple-element.7, f32[]{:T(128)S(6)} %sqrt.3, f32[512]{0:T(512)S(1)} %broadcast_multiply_fusion), kind=kLoop, calls=%fused_computation.18 | loop fusion | flops 1048576 | bytes 4196356 | tf_op jit(solution)/shard_map/div | solution.py:259
  157.3 2.8 %fusion.16 = f32[1,64,512]{2,1,0:T(8,128)} fusion(f32[512,1024]{1,0:T(8,128)S(1)} %subtract_divide_fusion, s32[]{:T(128)S(6)} %select_n.7, f32[64,1024]{1,0:T(8,128)S(1)} %constant_dynamic-slice_fusion, f32[]{:T(128)S(6)} %convert_element_type.19), kind=kOutput, calls=%fused_computation.21 | convolution fusion | flops 402685952 | bytes 2490376 | tf_op jit(solution)/shard_map/dot_general | solution.py:264
  (5 shorter events, 0.1 us)
Async XLA Ops:
  0.0 15.2 %copy-start.2 = (s32[16,128]{1,0:T(8,128)S(1)}, s32[16,128]{1,0:T(8,128)}, u32[]{:S(2)}) copy-start(s32[16,128]{1,0:T(8,128)} %param.4) | copy-start | bytes 24580
  6.1 3.3 %copy-start.1 = (f32[1024,16,128]{2,0,1:T(8,128)}, f32[1024,16,128]{2,0,1:T(8,128)S(1)}, u32[]{:S(2)}) copy-start(f32[1024,16,128]{2,0,1:T(8,128)S(1)} %copy.11) | copy-start | bytes 25165828
  9.5 15.0 %collective-permute-start = (f32[1024,1,128]{2,0,1:T(8,128)S(1)}, f32[1024,1,128]{2,0,1:T(8,128)S(1)}, u32[]{:S(2)}, u32[]{:S(2)}) collective-permute-start(f32[1024,1,128]{2,0,1:T(8,128)S(1)} %get-tuple-element.15), channel_id=1, source_target_pairs={{0,8},{8,16},{16,24},{24,32},{32,40},{40,48},{48,56},{56,64},{64,7... | collective-permute-start | bytes 1572872 | tf_op jit(solution)/shard_map/ppermute | solution.py:210
  13.9 16.4 %collective-permute-start.1 = (f32[1024,1,128]{2,0,1:T(8,128)S(1)}, f32[1024,1,128]{2,0,1:T(8,128)S(1)}, u32[]{:S(2)}, u32[]{:S(2)}) collective-permute-start(f32[1024,1,128]{2,0,1:T(8,128)S(1)} %get-tuple-element.14), channel_id=1, source_target_pairs={{8,0},{16,8},{24,16},{32,24},{40,32},{48,40},{56,48},{64,56},{72,6... | collective-permute-start | bytes 1572872 | tf_op jit(solution)/shard_map/ppermute | solution.py:211
  30.3 9.3 %copy-start = (f32[1024,18,128]{2,0,1:T(8,128)}, f32[1024,18,128]{2,0,1:T(8,128)S(1)}, u32[]{:S(2)}) copy-start(f32[1024,18,128]{2,0,1:T(8,128)S(1)} %constant_dynamic-update-slice_fusion) | copy-start | bytes 28311556
  45.2 12.3 %collective-permute-start.2 = (f32[1024,18,1]{0,2,1:T(1,128)S(1)}, f32[1024,18,1]{0,2,1:T(1,128)S(1)}, u32[]{:S(2)}, u32[]{:S(2)}) collective-permute-start(f32[1024,18,1]{0,2,1:T(1,128)S(1)} %copy.14), channel_id=1, source_target_pairs={{1,0},{2,1},{3,2},{4,3},{5,4},{6,5},{7,6},{9,8},{10,9},{11,10},{12... | collective-permute-start | bytes 221192 | tf_op jit(solution)/shard_map/ppermute | solution.py:211
  54.3 8.3 %collective-permute-start.3 = (f32[1024,18,1]{0,2,1:T(1,128)S(1)}, f32[1024,18,1]{0,2,1:T(1,128)S(1)}, u32[]{:S(2)}, u32[]{:S(2)}) collective-permute-start(f32[1024,18,1]{0,2,1:T(1,128)S(1)} %copy.16), channel_id=1, source_target_pairs={{0,1},{1,2},{2,3},{3,4},{4,5},{5,6},{6,7},{8,9},{9,10},{10,11},{11... | collective-permute-start | bytes 221192 | tf_op jit(solution)/shard_map/ppermute | solution.py:210

commit v2 on v1

--- a/solution.py
+++ b/solution.py
@@ -1,12 +1,21 @@
 import math
-
-from jax.sharding import PartitionSpec as P
 
 import jax
 import jax.numpy as jnp
 from jax import lax
 from jax.experimental import pallas as pl
 from jax.experimental.pallas import tpu as pltpu
+from jax.sharding import PartitionSpec as P
+
+LAG_DEV = 1
+
+
+GRAVITY = 9.81
+ROTATION = 7.2921e-05
+EARTH_RADIUS = 6371000.0
+LAT_SOUTH = 20.0
+LAT_SPAN = 45.0
+LON_STEP = 1.0 / 12.0
 
 MESH = pl.DeviceIdType.MESH
 
@@ -189,30 +198,6 @@
     )(tot, en)
 
 
-LAG_DEV = 1
-
-
-GRAVITY = 9.81
-ROTATION = 7.2921e-05
-EARTH_RADIUS = 6371000.0
-LAT_SOUTH = 20.0
-LAT_SPAN = 45.0
-LON_STEP = 1.0 / 12.0
-
-
-def padded_2(shard, sides, width):
-    for axis, dim in sides:
-        devices, length = (lax.axis_size(axis), shard.shape[dim])
-        up = [(i, (i + 1) % devices) for i in range(devices - 1)]
-        down = [(j, i) for i, j in up]
-        last = lax.slice_in_dim(shard, length - width, length, axis=dim)
-        initial = lax.slice_in_dim(shard, 0, width, axis=dim)
-        before = lax.ppermute(last, axis, up)
-        after = lax.ppermute(initial, axis, down)
-        shard = jnp.concatenate([before, shard, after], axis=dim)
-    return shard
-
-
 def stencil_coefs(rows_index, total_rows):
     degrees = LAT_SOUTH + LAT_SPAN * (rows_index.astype(jnp.float32) + 0.5) / total_rows
     radians = degrees * (math.pi / 180.0)
@@ -222,10 +207,137 @@
     return (-GRAVITY / (coriolis * 2.0 * north_step), GRAVITY / (coriolis * 2.0 * east_step))
 
 
-def velocities(padded, coef_east, coef_north, ocean):
-    lat_diff = padded[:, 1:-1, 2:] - padded[:, 1:-1, :-2]
-    lon_diff = padded[:, 2:, 1:-1] - padded[:, :-2, 1:-1]
-    return (coef_east * lat_diff * ocean, coef_north * lon_diff * ocean)
+DAYS, ROWS, COLS = 1024, 16, 128
+CHUNKS = 4
+STEP = 32
+
+
+def velocity_kernel(height, land, vel, energy, hs, south, north_halo, pack, west, east_halo,
+                    s_load, s_up, r_up, s_dn, r_dn, s_w, r_w, s_e, r_e):
+    lon = lax.axis_index("lon")
+    lat = lax.axis_index("lat")
+    per = DAYS // CHUNKS
+    up = ((lon + 1) % 32, lat)
+    down = ((lon + 31) % 32, lat)
+    right = (lon, (lat + 1) % 8)
+    left = (lon, (lat + 7) % 8)
+
+    loads = []
+    for n in range(CHUNKS):
+        for i in range(ROWS):
+            copy = pltpu.make_async_copy(height.at[pl.ds(n * per, per), i],
+                                         hs.at[i, pl.ds(n * per, per)], s_load.at[n * ROWS + i])
+            copy.start()
+            loads.append(copy)
+
+    barrier = pltpu.get_barrier_semaphore()
+    for dev in (up, down, right, left):
+        pl.semaphore_signal(barrier, inc=1, device_id=dev, device_id_type=MESH)
+    pl.semaphore_wait(barrier, 4)
+
+    pending = []
+
+    def send(src, dst, ssem, rsem, dev):
+        copy = pltpu.make_async_remote_copy(
+            src_ref=src, dst_ref=dst, send_sem=ssem, recv_sem=rsem,
+            device_id=dev, device_id_type=MESH)
+        copy.start()
+        pending.append(copy)
+        return copy
+
+    rows = []
+    for n in range(CHUNKS):
+        days = pl.ds(n * per, per)
+        a = send(height.at[days, ROWS - 1], south.at[days], s_up.at[n], r_up.at[n], up)
+        b = send(height.at[days, 0], north_halo.at[days], s_dn.at[n], r_dn.at[n], down)
+        rows.append((a, b))
+
+    lane = lax.broadcasted_iota(jnp.int32, (1, COLS), 1)
+    coef_east, coef_north = stencil_coefs(lat * COLS + lane, COLS * 8)
+    ocean = land[...].astype(jnp.float32)
+    ce = coef_east * ocean
+    cn = coef_north * ocean
+    lanes = lax.broadcasted_iota(jnp.int32, (STEP, COLS), 1)
+    inner = (lane > 0) & (lane < COLS - 1)
+    edge = (lanes == 0) | (lanes == COLS - 1)
+    group = lanes // 4
+    cb = jnp.zeros((1, COLS), jnp.float32)
+    for i in range(ROWS):
+        cb = jnp.where(lane // 4 == i, pltpu.roll(ce[i:i + 1], (4 * i + 2) % COLS, 1), cb)
+    has_right = lat < 7
+    has_left = lat > 0
+    has_up = lon < 31
+    has_down = lon > 0
+
+    cols = []
+    for n in range(CHUNKS):
+        for i in range(ROWS):
+            loads[n * ROWS + i].wait()
+
+        def pack_step(s, _):
+            at = pl.ds(pl.multiple_of(n * per + s * STEP, STEP), STEP)
+            packed = jnp.zeros((STEP, COLS), jnp.float32)
+            for i in range(ROWS):
+                packed = jnp.where(group == i, pltpu.roll(hs[i, at], (4 * i + 2) % COLS, 1), packed)
+            pack[at] = packed
+            return 0
+
+        lax.fori_loop(0, per // STEP, pack_step, 0)
+        days = pl.ds(n * per, per)
+        a = send(pack.at[days], west.at[days], s_w.at[n], r_w.at[n], right)
+        b = send(pack.at[days], east_halo.at[days], s_e.at[n], r_e.at[n], left)
+        cols.append((a, b))
+
+    total = jnp.zeros((8, COLS), jnp.float32)
+    for n in range(CHUNKS):
+        for copy in rows[n] + cols[n]:
+            copy.wait_recv()
+
+        def step(s, acc):
+            at = pl.ds(pl.multiple_of(n * per + s * STEP, STEP), STEP)
+            mine = pack[at]
+            from_right = jnp.where(has_right, east_halo[at], 0.0)
+            from_left = jnp.where(has_left, west[at], 0.0)
+            bound = jnp.where(
+                lanes % 4 == 1,
+                pltpu.roll(from_right, COLS - 1, 1) - pltpu.roll(mine, 1, 1),
+                pltpu.roll(mine, COLS - 1, 1) - pltpu.roll(from_left, 1, 1)) * cb
+            below = jnp.where(has_down, south[at], 0.0)
+            here = hs[0, at]
+            for i in range(ROWS):
+                above = hs[i + 1, at] if i < ROWS - 1 else jnp.where(has_up, north_halo[at], 0.0)
+                north = (above - below) * cn[i:i + 1]
+                diff = pltpu.roll(here, COLS - 1, 1) - pltpu.roll(here, 1, 1)
+                east = jnp.where(edge, pltpu.roll(bound, COLS - (4 * i + 2), 1), diff * ce[i:i + 1])
+                vel[0, i, at] = east.astype(jnp.bfloat16)
+                vel[1, i, at] = north.astype(jnp.bfloat16)
+                squares = east * east + north * north
+                for r in range(STEP // 8):
+                    acc = acc + squares[r * 8:r * 8 + 8]
+                below, here = here, above
+            return acc
+
+        total = lax.fori_loop(0, per // STEP, step, total)
+    energy[...] = total
+    for copy in pending:
+        copy.wait_send()
+
+
+def velocity(height, land_sea):
+    f32 = jnp.float32
+    vm = pl.BlockSpec(memory_space=pltpu.VMEM)
+    dma = pltpu.SemaphoreType.DMA
+    return pl.pallas_call(
+        velocity_kernel,
+        out_shape=[jax.ShapeDtypeStruct((2, ROWS, DAYS, COLS), jnp.bfloat16),
+                   jax.ShapeDtypeStruct((8, COLS), f32)],
+        in_specs=[pl.BlockSpec(memory_space=pl.ANY), vm],
+        out_specs=[vm, vm],
+        scratch_shapes=[pltpu.VMEM((ROWS, DAYS, COLS), f32)]
+        + [pltpu.VMEM((DAYS, COLS), f32)] * 5
+        + [dma((CHUNKS * ROWS,))] + [dma((CHUNKS,))] * 8,
+        compiler_params=pltpu.CompilerParams(collective_id=1, has_side_effects=True),
+    )(height, land_sea)
 
 
 def on_device(height, land_sea, patterns):
@@ -235,24 +347,11 @@
     total_rows = lat_cells * lat_devices
     lat_place = lax.axis_index("lat")
     lon_place = lax.axis_index("lon")
-    rows_index = lat_place * lat_cells + jnp.arange(lat_cells, dtype=jnp.int32)
-    coef_east, coef_north = stencil_coefs(rows_index, total_rows)
-    ocean = land_sea.astype(jnp.float32)
-    padded = padded_2(height, (("lon", 1), ("lat", 2)), 1)
-    east_vel, north_vel = velocities(padded, coef_east, coef_north, ocean)
-    local_energy = jnp.sum(east_vel * east_vel + north_vel * north_vel)
-    stacked = (
-        jnp.stack([east_vel, north_vel], axis=1)
-        .astype(jnp.bfloat16)
-        .reshape(days, 2 * lon_cells * lat_cells)
-    )
     mode_count = patterns.shape[0]
     owned = mode_count // lat_devices
-    flat_patterns = patterns.reshape(mode_count, 2 * lon_cells * lat_cells)
-    part = lax.dot_general(
-        flat_patterns, stacked, (((1,), (1,)), ((), ())), preferred_element_type=jnp.float32
-    )
-    totals, energies = allreduce(part, jnp.full((8, 128), local_energy * (1.0 / 1024.0)))
+    vel, tile = velocity(height, land_sea)
+    part = jnp.einsum("kcij,citj->kt", patterns, vel, preferred_element_type=jnp.float32)
+    totals, energies = allreduce(part, tile)
     energy = jnp.sum(energies)
     cell_total = 2.0 * days * lon_cells * lon_devices * total_rows
     centered = totals - jnp.mean(totals, axis=1, keepdims=True)

time: 161 us -> 93.8 us (0.58)
  local copies, waits for them, and re-layouts: 46.6 us -> 0.03 us
  Pallas kernels: 50.3 us -> 75.2 us
  other arithmetic: 26.8 us -> 4.2 us
  starting transfers between devices: 12.3 us -> 0 us
  waiting for transfers between devices: 9.23 us -> 0 us
    pallas_call x0 -> x1, Pallas kernels: none -> 30.1 us  [velocity(): pl.pallas_call(velocity_kernel, out_shape=[jax.ShapeDtypeStruct((2, ROWS,...]
    reduce_sum x1 -> x0, other arithmetic: 21.8 us -> none  [on_device(): local_energy = jnp.sum(east_vel * east_vel + north_vel * north_vel)]
    slice x4 -> x0, local copies, waits for them, and re-layouts: 19.7 us -> none  [the longest x3 14.1 us: padded_2(): initial = lax.slice_in_dim(shard, 0, width, axis=dim)]
    unnamed x9 -> x2, local copies, waits for them, and re-layouts: 16.1 us -> 0.01 us
    ppermute x4 -> x0, starting transfers between devices: 12.3 us -> none  [the longest x2 7.59 us: padded_2(): before = lax.ppermute(last, axis, up)]
    ppermute x2 -> x0, local copies, waits for them, and re-layouts: 10.2 us -> none  [the longest x1 5.13 us: padded_2(): before = lax.ppermute(last, axis, up)]
    ppermute x4 -> x0, waiting for transfers between devices: 9.23 us -> none  [the longest x2 9.22 us: padded_2(): before = lax.ppermute(last, axis, up)]
    pallas_call x1, Pallas kernels: 50.3 us -> 45.1 us  [allreduce(): pl.pallas_call(allreduce_kernel, out_shape=[jax.ShapeDtypeStruct((512, 10...]
  transfers between devices with their start and end apart: 4 -> 0, of which waited for: 1 -> 0; matrix products, arithmetic and copies ran while one was open for 10% -> 0% of each run, Pallas kernels for 0% -> 0%
where the time goes in v2:
time: 93.8 us; the launch traced here: 93.6 us
  Pallas kernels  75.2 us (80%)
  matrix products  13.4 us (14%)
  other arithmetic  4.2 us (4%)
    pallas_call x1, Pallas kernels, allreduce(): pl.pallas_call(allreduce_kernel, out_shape=[jax.ShapeDtypeStruct((512, 10...  45.1 us
    pallas_call x1, Pallas kernels, velocity(): pl.pallas_call(velocity_kernel, out_shape=[jax.ShapeDtypeStruct((2, ROWS,...  30.1 us
    dot_general x1, matrix products, on_device(): jnp.einsum('kcij,citj->kt', patterns, vel, preferred_element_type=jnp.flo...  10.6 us
    dot_general x1, matrix products, on_device(): lax.dot_general(shifted, normed, (((1,), (1,)), ((), ())), precision=lax....  2.83 us

profile of v2, /device:TPU:1, one launch (start us, length us, event | category | flops | bytes accessed | tf_op | source)
XLA Modules:
  0.0 93.6 jit_solution(5595373048085667463)
XLA Ops:
  0.0 30.1 %shard_map.37 = (bf16[2,16,1024,128]{3,2,1,0:T(8,128)(2,1)}, f32[8,128]{1,0:T(8,128)}) custom-call(f32[1024,16,128]{2,1,0:T(8,128)} %height.1, s32[16,128]{1,0:T(8,128)} %land.1), custom_call_target="tpu_custom_call" | custom-call | tf_op jit(solution)/shard_map/pallas_call | solution.py:330
  30.1 10.6 %fusion.2.tot = f32[512,1024]{1,0:T(8,128)} fusion(bf16[2,16,1024,128]{3,2,1,0:T(8,128)(2,1)} %get-tuple-element.9, bf16[512,2,16,128]{3,2,1,0:T(8,128)(2,1)} %param.5), kind=kOutput, calls=%fused_computation.3 | convolution fusion | flops 4294967296 | bytes 14680064 | tf_op jit(solution)/shard_map/kcij,citj->kt/dot_general | solution.py:353
  40.7 45.1 %shard_map.38 = (f32[512,1024]{1,0:T(8,128)}, f32[8,128]{1,0:T(8,128)}) custom-call(f32[512,1024]{1,0:T(8,128)} %fusion.2.tot, f32[8,128]{1,0:T(8,128)} %get-tuple-element.10.en), custom_call_target="tpu_custom_call" | custom-call | tf_op jit(solution)/shard_map/pallas_call | solution.py:177
  85.8 0.0 copy-start
  85.8 1.8 %reduce_sum.18 = f32[512]{0:T(512)S(1)} reduce(f32[512,1024]{1,0:T(8,128)} %get-tuple-element.11, f32[]{:T(128)} %constant.12.clone.1), dimensions={1}, to_apply=%region_0.0 | reduce | flops 523776 | bytes 2099204 | tf_op jit(solution)/shard_map/reduce_sum | solution.py:357
  87.6 0.0 copy-done
  87.6 0.6 reduce_sum.19
  88.9 1.8 %subtract_divide_fusion = f32[512,1024]{1,0:T(8,128)S(1)} fusion(f32[512,1024]{1,0:T(8,128)} %get-tuple-element.11, f32[]{:T(128)S(6)} %sqrt.3, f32[512]{0:T(512)S(1)} %broadcast_multiply_fusion), kind=kLoop, calls=%fused_computation.2 | loop fusion | flops 1048576 | bytes 4196356 | tf_op jit(solution)/shard_map/div | solution.py:358
  90.8 2.8 %fusion.5 = f32[1,64,512]{2,1,0:T(8,128)} fusion(f32[512,1024]{1,0:T(8,128)S(1)} %subtract_divide_fusion, s32[]{:T(128)S(6)} %select_n.7, f32[64,1024]{1,0:T(8,128)S(1)} %constant_dynamic-slice_fusion, f32[]{:T(128)S(6)} %convert_element_type.3), kind=kOutput, calls=%fused_computation.5 | convolution fusion | flops 402685952 | bytes 2490376 | tf_op jit(solution)/shard_map/dot_general | solution.py:363
  (2 shorter events, 0.0 us)
Async XLA Ops:
  85.8 1.8 %copy-start = (f32[8,128]{1,0:T(8,128)S(1)}, f32[8,128]{1,0:T(8,128)}, u32[]{:S(2)}) copy-start(f32[8,128]{1,0:T(8,128)} %get-tuple-element.12) | copy-start | bytes 12292
